TPU v7x, 512 devices: a whole 4x4x16 slice. The times are simulated.
512 devices in a mesh: row: 32 (over y, z_hi, core), col: 16 (over z_lo, x).
Axes of the slice: x: 4, y: 4, z: 16 (z_hi: 4, z_lo: 4; z = z_hi * 4 + z_lo), core: 2. Of those that a mesh axis runs over, the one named last changes fastest.
Arguments:
- forcing_terms: float32 [32, 16, 2, 32, 128], P('row', 'col'), may hold values from -6 to 6
- diagonal_reciprocal: float32 [32, 16, 2, 128, 128], P('row', 'col'), may hold values from -0.5 to 0.5
- stiffness_submatrix: float32 [32, 16, 32, 128, 128], P('row', 'col'), may hold values from -0.1875 to 0.1875
- stiffness_source_index: int32 [32, 16, 32], P('row', 'col'), may hold values from 0 to 31
- stiffness_target_index: int32 [32, 16, 32], P('row', 'col'), may hold values from 0 to 63
- stiffness_nonzero_tally: int32 [32, 16], P('row', 'col'), may hold values from 1 to 32, as said below
- interpolant_submatrix: float32 [32, 16, 16, 128, 128], P('row', 'col'), may hold values from -0.0625 to 0.0625
- interpolant_cluster_index: int32 [32, 16, 16], P('row', 'col'), may hold values from 0 to 1
- interpolant_target_index: int32 [32, 16, 16], P('row', 'col'), may hold values from 0 to 63
- interpolant_nonzero_tally: int32 [32, 16], P('row', 'col'), may hold values from 1 to 16, as said below
- provisional_interpolant: float32 [32, 16, 2, 128], P('row', 'col'), may hold values from 0.2 to 1
- cluster_label: int32 [32, 16, 2, 128], P('row', 'col'), may hold values from 0 to 255
Outputs:
- relaxed_iterate: float32 [32, 16, 2, 32, 128], P('row', 'col')
- residual: float32 [32, 16, 2, 32, 128], P('row', 'col')
- coarse: float32 [32, 2, 32, 128], P('row')
Inputs may be any that keep to these rules, and one draw needn't show every extreme that they name: `stiffness_nonzero_tally`: tile slots at or past the count are unused; some pair has all 32 slots live in every draw. `interpolant_nonzero_tally`: tile slots at or past the count are unused; some pair has all 16 slots live in every draw.
All inputs are finite; a program needn't handle non-finite values.
Results may differ from a plain program's by a relative error of at most 0.0003.
Values sent between devices are 32-bit elements; how exact they have to be, the bound alone decides.
No kernel may reach another device: no remote copies, remote signals or barrier semaphores. Data moves between devices by JAX's collectives and lax.ppermute only.
A program may use at most 64 MiB of HBM per device.

v0:
```python
import jax
import jax.numpy as jnp
from jax import lax
from jax.sharding import PartitionSpec as P

omega = 0.7
highest = lax.Precision.HIGHEST
tile_group = 8


def loop_tiles(blocks, stiffness_submatrices, rows, cols, low, high, nout):
    nrhs = blocks.shape[1]
    width = blocks.shape[2]

    def add_group(index, total):
        start = index * tile_group
        piece = lax.dynamic_slice_in_dim(stiffness_submatrices, start, tile_group, 0)
        row_ids = lax.dynamic_slice_in_dim(rows, start, tile_group, 0)
        col_ids = lax.dynamic_slice_in_dim(cols, start, tile_group, 0)
        slots = start + jnp.arange(tile_group)
        live = ((slots >= low) & (slots < high)).astype(jnp.float32)
        inputs = jnp.take(blocks, col_ids, axis=0)
        product = jnp.einsum("ska,sab->skb", inputs, piece, precision=highest)
        onehot = (row_ids[:, None] == jnp.arange(nout)[None, :]).astype(jnp.float32) * live[:, None]
        return total + jnp.einsum("so,skb->okb", onehot, product, precision=highest)

    starting_guess = low // tile_group
    last = (high + tile_group - 1) // tile_group
    empty = jnp.zeros((nout, nrhs, width), jnp.float32)
    return lax.fori_loop(starting_guess, last, add_group, empty)


def gather_columns(vec):
    whole = lax.all_gather(vec[None, None], "row", axis=0, tiled=True)
    return whole.reshape(-1, vec.shape[1], vec.shape[2])


def precondition(vec, inverse):
    return jnp.einsum("pka,pab->pkb", vec, inverse, precision=highest)


def stiffness_product(vec, stiffness_submatrices, rows, cols, count):
    blocks = gather_columns(vec)
    ncol = lax.axis_size("col")
    pblocks = vec.shape[0]
    nout = ncol * pblocks
    partial_value = loop_tiles(blocks, stiffness_submatrices, rows, cols, jnp.int32(0), count, nout)
    partial_value = partial_value.reshape(1, ncol, pblocks, vec.shape[1], vec.shape[2])
    summed = lax.psum_scatter(partial_value, "col", scatter_dimension=1, tiled=True)
    return summed[0, 0]


def body(
    forcing_terms,
    diagonal_reciprocal,
    stiffness_submatrix,
    stiffness_source_index,
    stiffness_target_index,
    stiffness_nonzero_tally,
    interpolant_submatrix,
    interpolant_cluster_index,
    interpolant_target_index,
    interpolant_nonzero_tally,
    provisional_interpolant,
    cluster_label,
):
    source = forcing_terms[0, 0]
    inverse = diagonal_reciprocal[0, 0]
    stiffness_submatrices = stiffness_submatrix[0, 0]
    rows = stiffness_source_index[0, 0]
    cols = stiffness_target_index[0, 0]
    count = stiffness_nonzero_tally[0, 0]
    starting_guess = omega * precondition(source, inverse)
    image_field = stiffness_product(starting_guess, stiffness_submatrices, rows, cols, count)
    relaxed_iterate = starting_guess + omega * precondition(source - image_field, inverse)
    image_field = stiffness_product(relaxed_iterate, stiffness_submatrices, rows, cols, count)
    residual = source - image_field
    pblocks, nrhs, width = residual.shape
    blocks = gather_columns(residual)
    part = loop_tiles(
        blocks,
        interpolant_submatrix[0, 0],
        interpolant_cluster_index[0, 0],
        interpolant_target_index[0, 0],
        jnp.int32(0),
        interpolant_nonzero_tally[0, 0],
        pblocks,
    )
    weighted = (
        (residual * provisional_interpolant[0, 0][:, None, :])
        .transpose(1, 0, 2)
        .reshape(nrhs, pblocks * width)
    )
    onehot = (
        cluster_label[0, 0].reshape(-1)[:, None] == jnp.arange(pblocks * width)[None, :]
    ).astype(jnp.float32)
    tentative = jnp.dot(weighted, onehot, precision=highest)
    part = part + tentative.reshape(nrhs, pblocks, width).transpose(1, 0, 2)
    coarse = lax.psum(part, "col")
    return (relaxed_iterate[None, None], residual[None, None], coarse[None])


def solution(mesh):
    placed = (
        P("row", "col", None, None, None),
        P("row", "col", None, None, None),
        P("row", "col", None, None, None),
        P("row", "col", None),
        P("row", "col", None),
        P("row", "col"),
        P("row", "col", None, None, None),
        P("row", "col", None),
        P("row", "col", None),
        P("row", "col"),
        P("row", "col", None, None),
        P("row", "col", None, None),
    )
    return jax.shard_map(
        body,
        mesh=mesh,
        in_specs=placed,
        out_specs=(
            P("row", "col", None, None, None),
            P("row", "col", None, None, None),
            P("row", None, None, None),
        ),
        check_vma=False,
    )
```

profile of v0, /device:TPU:24, one launch (start us, length us, event | category | flops | bytes accessed | tf_op | source)
XLA Modules:
  0.0 539.5 jit_solution(16684769150870673594)
XLA Ops:
  7.2 0.8 copy-done
  8.1 1.6 convolution_multiply_fusion.1
  10.4 75.4 %all-gather.8.cloned.1.call-done = f32[64,32,128]{2,1,0:T(8,128)} async-done(((f32[2,32,128]{2,1,0:T(8,128)}), f32[64,32,128]{2,1,0:T(8,128)}) %all-gather.8.cloned.1.call-update) | async-done | bytes 1048592 | tf_op jit(solution)/shard_map/all_gather | solution.py:34
  85.9 25.5 %while.30 = (s32[]{:T(128)}, f32[32,32,128]{2,0,1:T(8,128)S(1)}, s32[]{:T(128)}, s32[32]{0:T(128)}, s32[]{:T(128)}, /*index=5*/s32[32]{0:T(128)}, f32[64,32,128]...) while((s32[]{:T(128)}, f32[32,32,128]{2,0,1:T(8,128)S(1)}, ...), condition=%wide.region_1.3_spmd, body=%wide.region_0.2_spmd.sunk | while | flops 63080028 | bytes 2232807 | solution.py:30
  85.9 1.4 compare_and_fusion.6
  87.3 1.8 gather_fusion
  89.1 1.7 fusion.75
  90.7 0.7 dynamic_slice.46
  91.4 0.8 convolution_add_fusion.6
  92.3 1.4 compare_and_fusion.6
  93.7 1.8 gather_fusion
  95.4 1.7 fusion.75
  97.1 0.7 dynamic_slice.46
  97.8 0.8 convolution_add_fusion.6
  98.6 1.4 compare_and_fusion.6
  100.0 1.8 gather_fusion
  101.8 1.7 fusion.75
  103.5 0.7 dynamic_slice.46
  104.2 0.8 convolution_add_fusion.6
  105.0 1.4 compare_and_fusion.6
  106.4 1.8 gather_fusion
  108.2 1.7 fusion.75
  109.9 0.7 dynamic_slice.46
  110.6 0.8 convolution_add_fusion.6
  111.4 1.1 copy.25
  112.6 86.0 %reduce-scatter.3.cloned.1.call-done = f32[1,1,2,32,128]{4,3,2,1,0:T(8,128)} async-done(((f32[1,16,2,32,128]{4,3,2,1,0:T(8,128)}), f32[1,1,2,32,128]{4,3,2,1,0:T(8,128)}) %reduce-scatter.3.cloned.1.call-update) | async-done | bytes 32784 | tf_op jit(solution)/shard_map/reduce_scatter | solution.py:49
  198.6 1.6 fusion.45
  200.3 68.1 %all-gather.10.cloned.1.call-done = f32[64,32,128]{2,1,0:T(8,128)} async-done(((f32[2,32,128]{2,1,0:T(8,128)}), f32[64,32,128]{2,1,0:T(8,128)}) %all-gather.10.cloned.1.call-update) | async-done | bytes 1048592 | tf_op jit(solution)/shard_map/all_gather | solution.py:34
  268.5 20.4 %while.31 = (s32[]{:T(128)}, f32[32,32,128]{2,0,1:T(8,128)S(1)}, s32[]{:T(128)}, s32[32]{0:T(128)S(1)}, s32[]{:T(128)}, /*index=5*/s32[32]{0:T(128)S(1)}, f32[64...) while((s32[]{:T(128)}, f32[32,32,128]{2,0,1:T(8,128)S(1)}, ...), condition=%wide.region_4.6_spmd, body=%wide.region_3.5_spmd.sunk | while | flops 63080028 | bytes 2232807 | solution.py:30
  268.6 0.8 compare_and_fusion.7
  269.4 1.8 gather_fusion.1
  271.2 1.7 fusion.80
  272.8 0.1 dynamic_slice.48
  272.9 0.8 convolution_add_fusion.7
  273.7 0.7 compare_and_fusion.7
  274.5 1.8 gather_fusion.1
  276.2 1.7 fusion.80
  277.9 0.1 dynamic_slice.48
  278.0 0.8 convolution_add_fusion.7
  278.8 0.7 compare_and_fusion.7
  279.5 1.8 gather_fusion.1
  281.3 1.7 fusion.80
  283.0 0.8 convolution_add_fusion.7
  283.9 0.7 compare_and_fusion.7
  284.6 1.8 gather_fusion.1
  286.4 1.7 fusion.80
  288.1 0.8 convolution_add_fusion.7
  288.9 1.1 copy.26
  290.1 85.9 %reduce-scatter.5.cloned.1.call-done = f32[1,1,2,32,128]{4,3,2,1,0:T(8,128)} async-done(((f32[1,16,2,32,128]{4,3,2,1,0:T(8,128)}), f32[1,1,2,32,128]{4,3,2,1,0:T(8,128)}) %reduce-scatter.5.cloned.1.call-update) | async-done | bytes 32784 | tf_op jit(solution)/shard_map/reduce_scatter | solution.py:49
  376.1 1.4 sub.30
  378.1 0.8 fusion.52
  379.0 66.8 %all-gather.6.cloned.1.call-done = f32[32,1,2,32,128]{4,3,2,1,0:T(8,128)} async-done(((f32[1,1,2,32,128]{4,3,2,1,0:T(8,128)}), f32[32,1,2,32,128]{4,3,2,1,0:T(8,128)}) %all-gather.6.cloned.1.call-update) | async-done | bytes 1048592 | tf_op jit(solution)/shard_map/all_gather | solution.py:34
  445.8 7.1 %while.32 = (s32[]{:T(128)}, f32[2,32,128]{2,0,1:T(2,128)S(1)}, s32[]{:T(128)}, s32[16]{0:T(128)S(1)}, s32[]{:T(128)}, /*index=5*/s32[16]{0:T(128)S(1)}, f32[64,...) while((s32[]{:T(128)}, f32[2,32,128]{2,0,1:T(2,128)S(1)}, ...), condition=%wide.region_7.9_spmd, body=%wide.region_6.8_spmd.sunk | while | flops 51160188 | bytes 1250271 | solution.py:30
  445.8 0.7 compare_and_fusion.8
  446.6 1.8 gather_fusion.2
  448.4 0.6 fusion.85
  449.0 0.1 dynamic_slice.50
  449.0 0.3 convolution_add_fusion.8
  449.4 0.7 compare_and_fusion.8
  450.1 1.8 gather_fusion.2
  451.9 0.6 fusion.85
  452.6 0.3 convolution_add_fusion.8
  453.0 0.3 fusion.44
  453.3 79.7 %psum.7 = f32[1,2,32,128]{3,2,1,0:T(8,128)} all-reduce(f32[1,2,32,128]{3,2,1,0:T(8,128)S(1)} %fusion.44), channel_id=1, replica_groups=mesh['row'=32,'col'=16] {'col'}, use_global_device_ids=true, to_apply=%region_8.10 | all-reduce | flops 8192 | bytes 65536 | tf_op jit(solution)/shard_map/psum | solution.py:99
  (48 shorter events, 0.8 us)
Async XLA Ops:
  7.2 0.9 copy-start
  7.2 78.6 %all-gather.8.cloned.1.call-start = ((), (), s32[]{:S(2)}) async-start(), calls=%async_computation.5 | async-start | bytes 1081344 | tf_op jit(solution)/shard_map/all_gather | solution.py:34
  9.7 188.9 %reduce-scatter.3.cloned.1.call-start = ((), (), s32[]{:S(2)}) async-start(), calls=%async_computation.2 | async-start | bytes 557056 | tf_op jit(solution)/shard_map/reduce_scatter | solution.py:49
  85.8 112.8 %copy-start.2 = (f32[1,1,2,32,128]{4,3,2,1,0:T(8,128)S(1)}, f32[1,1,2,32,128]{4,3,2,1,0:T(8,128)}, u32[]{:S(2)}) copy-start(f32[1,1,2,32,128]{4,3,2,1,0:T(8,128)} %param.20) | copy-start | bytes 98308
  85.9 112.8 %copy-start.3 = (f32[2,32,128]{2,1,0:T(8,128)S(1)}, f32[2,32,128]{2,1,0:T(8,128)}, u32[]{:S(2)}) copy-start(f32[2,32,128]{2,1,0:T(8,128)} %convolution_multiply_fusion.1) | copy-start | bytes 98308
  111.4 157.1 %copy-start.4 = (s32[32]{0:T(128)S(1)}, s32[32]{0:T(128)}, u32[]{:S(2)}) copy-start(s32[32]{0:T(128)} %get-tuple-element.489) | copy-start | bytes 388
  111.4 157.1 %copy-start.8 = (s32[32]{0:T(128)S(1)}, s32[32]{0:T(128)}, u32[]{:S(2)}) copy-start(s32[32]{0:T(128)} %get-tuple-element.491) | copy-start | bytes 388
  112.6 155.9 %all-gather.10.cloned.1.call-start = ((), (), s32[]{:S(2)}) async-start(), calls=%async_computation.6 | async-start | bytes 1081344 | tf_op jit(solution)/shard_map/all_gather | solution.py:34
  200.2 175.8 %reduce-scatter.5.cloned.1.call-start = ((), (), s32[]{:S(2)}) async-start(), calls=%async_computation.3 | async-start | bytes 557056 | tf_op jit(solution)/shard_map/reduce_scatter | solution.py:49
  268.5 109.6 %copy-start.6 = (f32[1,1,2,128]{3,2,1,0:T(2,128)S(1)}, f32[1,1,2,128]{3,2,1,0:T(2,128)}, u32[]{:S(2)}) copy-start(f32[1,1,2,128]{3,2,1,0:T(2,128)} %param.30) | copy-start | bytes 3076
  268.5 177.3 %copy-start.1 = (f32[1,1,16,128,128]{4,3,2,1,0:T(8,128)S(1)}, f32[1,1,16,128,128]{4,3,2,1,0:T(8,128)}, u32[]{:S(2)}) copy-start(f32[1,1,16,128,128]{4,3,2,1,0:T(8,128)} %param.26) | copy-start | bytes 3145732
  268.5 177.3 %copy-start.5 = (s32[1,1,16]{2,1,0:T(1,128)S(1)}, s32[1,1,16]{2,1,0:T(1,128)}, u32[]{:S(2)}) copy-start(s32[1,1,16]{2,1,0:T(1,128)} %param.28) | copy-start | bytes 196
  268.5 177.3 %copy-start.9 = (s32[1,1,16]{2,1,0:T(1,128)S(1)}, s32[1,1,16]{2,1,0:T(1,128)}, u32[]{:S(2)}) copy-start(s32[1,1,16]{2,1,0:T(1,128)} %param.27) | copy-start | bytes 196
  290.1 155.7 %all-gather.6.cloned.1.call-start = ((), (), s32[]{:S(2)}) async-start(), calls=%async_computation.4 | async-start | bytes 1081344 | tf_op jit(solution)/shard_map/all_gather | solution.py:34
  445.8 7.2 %copy-start.7 = (s32[1,1,2,128]{3,2,1,0:T(2,128)S(1)}, s32[1,1,2,128]{3,2,1,0:T(2,128)}, u32[]{:S(2)}) copy-start(s32[1,1,2,128]{3,2,1,0:T(2,128)} %param.31) | copy-start | bytes 3076
Sparse Core Ops, SparseCore 0:
  11.7 74.0 all-gather.7
  112.7 85.8 reduce-scatter.2
  202.3 66.0 all-gather.9
  290.2 85.8 reduce-scatter.4
  379.6 66.1 all-gather.5
where the time goes:
time: 541 us; the launch traced here: 540 us
  waiting for transfers between devices  382 us (71%)
  blocking collectives  79.7 us (15%)
  matrix products  25 us (5%)
  local copies, waits for them, and re-layouts  24.5 us (5%)
  between operations  15.3 us (3%)
  other arithmetic  12.2 us (2%)
    all_gather x3, waiting for transfers between devices, gather_columns(): whole = lax.all_gather(vec[None, None], 'row', axis=0, tiled=True)  210 us
    reduce_scatter x2, waiting for transfers between devices, stiffness_product(): lax.psum_scatter(partial_value, 'col', scatter_dimension=1, tiled=True)  172 us
    psum x1, blocking collectives, body(): coarse = lax.psum(part, 'col')  79.7 us
    gather x10, local copies, waits for them, and re-layouts, add_group(): inputs = jnp.take(blocks, col_ids, axis=0)  17.8 us
    dot_general x10, matrix products, add_group(): product = jnp.einsum('ska,sab->skb', inputs, piece, precision=highest)  14.4 us
  transfers between devices with their start and end apart: 5, of which 5 were waited for; matrix products, arithmetic and copies ran while one was open for 0% of the time, Pallas kernels for 0%

commit v1 on v0

v1 whole, which is shorter than its diff:
```python
import functools

import jax
import jax.numpy as jnp
from jax import lax
from jax.experimental import pallas as pl
from jax.experimental.pallas import tpu as pltpu
from jax.sharding import Mesh, PartitionSpec as P

omega = 0.7
unroll = 4
f32 = jnp.float32
bf16 = jnp.bfloat16


def split(v):
    high = v.astype(bf16)
    return high, (v - high.astype(f32)).astype(bf16)


def product(x, w):
    n, m = x.shape[0], w.shape[1]
    left = jnp.concatenate(split(x), axis=0)
    right = jnp.concatenate(split(w), axis=1)
    full = jnp.dot(left, right, preferred_element_type=f32)
    small = full[:n, m:] + full[n:, :m] + full[n:, m:]
    return full[:n, :m] + small


def spread(ref, value, p):
    for copy in range(ref.shape[0]):
        ref[copy, p] = value


def first_kernel(source, inverse, first, copies):
    for p in range(source.shape[0]):
        value = omega * product(source[p], inverse[p])
        first[p] = value
        spread(copies, value, p)


def column_sum(parts, p):
    total = parts[0, p]
    for j in range(1, parts.shape[0]):
        total = total + parts[j, p]
    return total


def relax_kernel(source, inverse, first, parts, relaxed, copies):
    for p in range(source.shape[0]):
        image = column_sum(parts, p)
        value = first[p] + omega * product(source[p] - image, inverse[p])
        relaxed[p] = value
        spread(copies, value, p)


def residual_kernel(source, parts, weights, labels, residual, copies, tentative):
    pblocks, nrhs, width = source.shape
    total = jnp.zeros((nrhs, pblocks * width), f32)
    for p in range(pblocks):
        value = source[p] - column_sum(parts, p)
        residual[p] = value
        spread(copies, value, p)
        weighted = value * weights[p : p + 1, :]
        aggregate = lax.broadcasted_iota(jnp.int32, (pblocks * width, width), 0)
        member = (aggregate == labels[p : p + 1, :]).astype(f32).astype(bf16)
        high, rest = split(weighted)
        low = (weighted - high.astype(f32) - rest.astype(f32)).astype(bf16)
        stacked = jnp.concatenate([high, rest, low, low], axis=0)
        spreadsum = lax.dot_general(
            stacked, member, (((1,), (1,)), ((), ())), preferred_element_type=f32
        )
        total = total + (
            spreadsum[:nrhs]
            + (spreadsum[nrhs : 2 * nrhs] + spreadsum[2 * nrhs : 3 * nrhs])
        )
    for p in range(pblocks):
        tentative[p] = total[:, p * width : (p + 1) * width]


def sum_kernel(parts, out):
    for p in range(out.shape[0]):
        out[p] = column_sum(parts, p)


def tile_kernel(core, count, rows, cols, own, other, tiles, start, out):
    nout = out.shape[0]
    nsource = own.shape[0]
    capacity = tiles.shape[0]
    live_count = count[0]
    mine = core[0]
    if start is None:
        out[...] = jnp.zeros_like(out)
    else:
        out[...] = start[...]

    def group(g, carry):
        terms = []
        for u in range(unroll):
            slot = g * unroll + u
            live = slot < live_count
            target = jnp.clip(cols[slot], 0, 2 * nsource - 1)
            index = (target // 4) * 2 + target % 2
            same = (target // 2) % 2 == mine
            x = jnp.where(same, own[index], other[index])
            x = jnp.where(live, x, 0.0)
            terms.append((jnp.clip(rows[slot], 0, nout - 1), product(x, tiles[slot])))
        for row, term in terms:
            out[row] = out[row] + term
        return carry

    lax.fori_loop(0, (live_count + unroll - 1) // unroll, group, 0)


def vmem(n):
    return [pl.BlockSpec(memory_space=pltpu.VMEM)] * n


def smem(n):
    return [pl.BlockSpec(memory_space=pltpu.SMEM)] * n


def call(kernel, name, shapes, *args):
    return pl.pallas_call(
        kernel,
        out_shape=tuple(jax.ShapeDtypeStruct(s, f32) for s in shapes),
        in_specs=vmem(len(args)),
        out_specs=tuple(vmem(len(shapes))),
        name=name,
    )(*args)


def tile_terms(name, core, count, rows, cols, own, other, tiles, start, nout):
    block = own.shape[1:]
    extra = () if start is None else (start,)

    def kernel(core, count, rows, cols, own, other, tiles, *rest):
        tile_kernel(core, count, rows, cols, own, other, tiles,
                    None if start is None else rest[0], rest[-1])

    return pl.pallas_call(
        kernel,
        out_shape=jax.ShapeDtypeStruct((nout,) + block, f32),
        in_specs=smem(4) + vmem(3 + len(extra)),
        out_specs=pl.BlockSpec(memory_space=pltpu.VMEM),
        name=name,
    )(core, count, rows, cols, own, other, tiles, *extra)


def gather_rows(copies):
    nz, ny = lax.axis_size("zh"), lax.axis_size("y")
    block = copies.shape[2:]
    planes = lax.all_to_all(copies, "zh", 0, 0, tiled=True)
    slab = lax.optimization_barrier(
        jnp.broadcast_to(planes[None], (ny,) + planes.shape)
    )
    own = lax.all_to_all(slab, "y", 0, 0, tiled=True).reshape((-1,) + block)
    other = lax.ppermute(own, "core", [(0, 1), (1, 0)])
    return own, other


def sum_columns(partial, pblocks):
    chunks = partial.reshape((-1, pblocks) + partial.shape[1:])
    return lax.all_to_all(chunks, ("zl", "x"), 0, 0, tiled=True)


def body(
    forcing_terms,
    diagonal_reciprocal,
    stiffness_submatrix,
    stiffness_source_index,
    stiffness_target_index,
    stiffness_nonzero_tally,
    interpolant_submatrix,
    interpolant_cluster_index,
    interpolant_target_index,
    interpolant_nonzero_tally,
    provisional_interpolant,
    cluster_label,
):
    source = forcing_terms[0, 0]
    inverse = diagonal_reciprocal[0, 0]
    tiles = stiffness_submatrix[0, 0]
    rows = stiffness_source_index[0, 0]
    cols = stiffness_target_index[0, 0]
    count = stiffness_nonzero_tally[0]
    core = lax.axis_index("core").astype(jnp.int32).reshape(1)
    pblocks = source.shape[0]
    ncol = lax.axis_size(("zl", "x"))
    nz = lax.axis_size("zh")
    block = source.shape
    spreads = (nz,) + block

    first, copies = call(first_kernel, "first", (block, spreads), source, inverse)
    own, other = gather_rows(copies)
    partial = tile_terms("image1", core, count, rows, cols, own, other, tiles, None, ncol * pblocks)
    parts = sum_columns(partial, pblocks)
    relaxed, copies = call(
        relax_kernel, "relax", (block, spreads), source, inverse, first, parts
    )
    own, other = gather_rows(copies)
    partial = tile_terms("image2", core, count, rows, cols, own, other, tiles, None, ncol * pblocks)
    parts = sum_columns(partial, pblocks)
    residual, copies, tentative = call(
        residual_kernel,
        "residual",
        (block, spreads, block),
        source,
        parts,
        provisional_interpolant[0, 0],
        cluster_label[0, 0],
    )
    own, other = gather_rows(copies)
    share = tile_terms(
        "restrict",
        core,
        interpolant_nonzero_tally[0],
        interpolant_cluster_index[0, 0],
        interpolant_target_index[0, 0],
        own,
        other,
        interpolant_submatrix[0, 0],
        tentative,
        pblocks,
    )
    shares = lax.optimization_barrier(jnp.broadcast_to(share[None], (ncol,) + block))
    shares = lax.all_to_all(shares, ("zl", "x"), 0, 0, tiled=True)
    (coarse,) = call(sum_kernel, "coarse", (block,), shares)
    return (relaxed[None, None], residual[None, None], coarse[None])


def solution(mesh):
    grid = Mesh(mesh.devices.reshape(4, 4, 2, 4, 4), ("y", "zh", "core", "zl", "x"))
    row = ("y", "zh", "core")
    col = ("zl", "x")
    spec = P(row, col)
    return jax.shard_map(
        body,
        mesh=grid,
        in_specs=(spec,) * 12,
        out_specs=(spec, spec, P(row)),
        check_vma=False,
    )
```

time: 541 us -> 197 us (0.36)
  waiting for transfers between devices: 382 us -> 4.33 us
  blocking collectives: 79.7 us -> 163 us
  matrix products: 25 us -> 0 us
  local copies, waits for them, and re-layouts: 24.5 us -> 3.37 us
  Pallas kernels: 0 us -> 16 us
  between operations: 15.3 us -> 2 us
  other arithmetic: 12.2 us -> 0 us
  starting transfers between devices: 0.2 us -> 5.73 us
    all_gather x3 -> x0, waiting for transfers between devices: 210 us -> none  [gather_columns(): whole = lax.all_gather(vec[None, None], 'row', axis=0, tiled=True)]
    reduce_scatter x2 -> x0, waiting for transfers between devices: 172 us -> none  [stiffness_product(): lax.psum_scatter(partial_value, 'col', scatter_dimension=1, tiled=True)]
    all_to_all x0 -> x9, blocking collectives: none -> 163 us  [the longest x3 65 us: gather_rows(): planes = lax.all_to_all(copies, 'zh', 0, 0, tiled=True)]
    psum x1 -> x0, blocking collectives: 79.7 us -> none  [body(): coarse = lax.psum(part, 'col')]
    dot_general x23 -> x0, matrix products: 25 us -> none  [the longest x10 14.4 us: add_group(): product = jnp.einsum('ska,sab->skb', inputs, piece, precision=highest)]
    gather x10 -> x0, local copies, waits for them, and re-layouts: 17.8 us -> none  [add_group(): inputs = jnp.take(blocks, col_ids, axis=0)]
    pallas_call x0 -> x7, Pallas kernels: none -> 16 us  [the longest x3 8.7 us: tile_terms(): pl.pallas_call(kernel, out_shape=jax.ShapeDtypeStruct((nout,) + block, f3...]
    and x10 -> x0, other arithmetic: 9.98 us -> none  [add_group(): inputs = jnp.take(blocks, col_ids, axis=0)]
  transfers between devices with their start and end apart: 5 -> 3, of which waited for: 5 -> 3; matrix products, arithmetic and copies ran while one was open for 0% -> 0% of each run, Pallas kernels for 0% -> 0%
where the time goes in v1:
time: 197 us; the launch traced here: 194 us
  blocking collectives  163 us (83%)
  Pallas kernels  16 us (8%)
  starting transfers between devices  5.73 us (3%)
  waiting for transfers between devices  4.33 us (2%)
  local copies, waits for them, and re-layouts  3.37 us (2%)
  between operations  2 us (1%)
    all_to_all x3, blocking collectives, gather_rows(): planes = lax.all_to_all(copies, 'zh', 0, 0, tiled=True)  65 us
    all_to_all x2, blocking collectives, sum_columns(): return lax.all_to_all(chunks, ('zl', 'x'), 0, 0, tiled=True)  44.6 us
    all_to_all x3, blocking collectives, gather_rows(): own = lax.all_to_all(slab, 'y', 0, 0, tiled=True).reshape((-1,) + block)  33.4 us
    all_to_all x1, blocking collectives, body(): shares = lax.all_to_all(shares, ('zl', 'x'), 0, 0, tiled=True)  20.1 us
    pallas_call x3, Pallas kernels, tile_terms(): pl.pallas_call(kernel, out_shape=jax.ShapeDtypeStruct((nout,) + block, f3...  8.7 us
    pallas_call x4, Pallas kernels, call(): pl.pallas_call(kernel, out_shape=tuple((jax.ShapeDtypeStruct(s, f32) for...  7.26 us
    ppermute x3, starting transfers between devices, gather_rows(): other = lax.ppermute(own, 'core', [(0, 1), (1, 0)])  5.73 us
    ppermute x3, waiting for transfers between devices, gather_rows(): other = lax.ppermute(own, 'core', [(0, 1), (1, 0)])  4.33 us
  transfers between devices with their start and end apart: 3, of which 3 were waited for; matrix products, arithmetic and copies ran while one was open for 0% of the time, Pallas kernels for 0%

profile of v1, /device:TPU:24, one launch (start us, length us, event | category | flops | bytes accessed | tf_op | source)
XLA Modules:
  0.0 194.5 jit_solution(2319078216349896463)
XLA Ops:
  0.6 1.7 first.1
  2.4 29.5 %all_to_all.45 = f32[4,2,32,128]{3,2,1,0:T(8,128)S(1)} all-to-all(f32[4,2,32,128]{3,2,1,0:T(8,128)} %get-tuple-element.11), channel_id=1, replica_groups=mesh['y'=4,'zh'=4,'core'=2,'zl'=4,'x'=4] {'zh'}, dimensions={0} | all-to-all | bytes 262144 | tf_op jit(solution)/shard_map/all_to_all | solution.py:153
  32.0 10.5 %all_to_all.46 = f32[4,4,2,32,128]{4,3,2,1,0:T(8,128)S(1)} all-to-all(f32[4,4,2,32,128]{4,3,2,1,0:T(8,128)S(1)} %broadcast_in_dim.14), channel_id=1, replica_groups=mesh['y'=4,'zh'=4,'core'=2,'zl'=4,'x'=4] {'y'}, dimensions={0} | all-to-all | bytes 1048576 | tf_op jit(solution)/shard_map/all_to_all | solution.py:157
  42.5 0.0 copy-start
  42.5 1.9 collective-permute-start
  45.0 1.2 collective-permute-done.other
  46.3 0.0 copy-start.3
  46.3 0.0 copy-done
  46.3 0.8 copy-done.3
  47.1 3.2 %image1.1 = f32[32,32,128]{2,1,0:T(8,128)} custom-call(s32[1]{0:T(128)} %bitcast.2.core, s32[1]{0:T(128)} %bitcast.21.count, s32[32]{0:T(128)} %bitcast.41, s32[32]{0:T(128)} %bitcast.43, f32[32,32,128]{2,1,0:T(8,128)} %bitcast.27, f32[32,32,128]{2,1,0:T(8,128)} %copy-done.3, f32[32,128,128]{2,1,0:T(8,128)} %bitcast.24), custom_call_target="tpu_custom_call" | custom-call | tf_op jit(solution)/shard_map/image1/pallas_call | solution.py:141
  50.2 23.0 %all_to_all.47.parts = f32[16,2,32,128]{3,2,1,0:T(8,128)} all-to-all(f32[16,2,32,128]{3,2,1,0:T(8,128)} %bitcast.33), channel_id=1, replica_groups=mesh['y'=4,'zh'=4,'core'=2,'zl'=4,'x'=4] {'zl','x'}, dimensions={0} | all-to-all | bytes 1048576 | tf_op jit(solution)/shard_map/all_to_all | solution.py:164
  73.2 2.0 %relax.1 = (f32[2,32,128]{2,1,0:T(8,128)}, f32[4,2,32,128]{3,2,1,0:T(8,128)}) custom-call(f32[2,32,128]{2,1,0:T(8,128)} %bitcast.38, f32[2,128,128]{2,1,0:T(8,128)} %bitcast.36, f32[2,32,128]{2,1,0:T(8,128)} %get-tuple-element.10.first, f32[16,2,32,128]{3,2,1,0:T(8,128)} %all_to_all.47.parts), custom_call_target="tpu_custom_call" | custom-call | tf_op jit(solution)/shard_map/relax/pallas_call | solution.py:124
  75.2 17.6 %all_to_all.48 = f32[4,2,32,128]{3,2,1,0:T(8,128)S(1)} all-to-all(f32[4,2,32,128]{3,2,1,0:T(8,128)} %get-tuple-element.13), channel_id=1, replica_groups=mesh['y'=4,'zh'=4,'core'=2,'zl'=4,'x'=4] {'zh'}, dimensions={0} | all-to-all | bytes 262144 | tf_op jit(solution)/shard_map/all_to_all | solution.py:153
  92.9 11.5 %all_to_all.49 = f32[4,4,2,32,128]{4,3,2,1,0:T(8,128)S(1)} all-to-all(f32[4,4,2,32,128]{4,3,2,1,0:T(8,128)S(1)} %broadcast_in_dim.16), channel_id=1, replica_groups=mesh['y'=4,'zh'=4,'core'=2,'zl'=4,'x'=4] {'y'}, dimensions={0} | all-to-all | bytes 1048576 | tf_op jit(solution)/shard_map/all_to_all | solution.py:157
  104.4 0.0 copy-start.2
  104.4 1.9 collective-permute-start.1
  106.3 1.9 collective-permute-done.1.other
  108.2 0.0 copy-start.5
  108.2 0.0 copy-done.2
  108.2 0.8 copy-done.5
  109.0 3.2 %image2.1 = f32[32,32,128]{2,1,0:T(8,128)} custom-call(s32[1]{0:T(128)} %bitcast.2.core, s32[1]{0:T(128)} %bitcast.22.count, s32[32]{0:T(128)} %bitcast.42, s32[32]{0:T(128)} %bitcast.44, f32[32,32,128]{2,1,0:T(8,128)} %bitcast.31, f32[32,32,128]{2,1,0:T(8,128)} %copy-done.5, f32[32,128,128]{2,1,0:T(8,128)} %bitcast.25), custom_call_target="tpu_custom_call" | custom-call | tf_op jit(solution)/shard_map/image2/pallas_call | solution.py:141
  112.2 21.6 %all_to_all.50.parts = f32[16,2,32,128]{3,2,1,0:T(8,128)} all-to-all(f32[16,2,32,128]{3,2,1,0:T(8,128)} %bitcast.32), channel_id=1, replica_groups=mesh['y'=4,'zh'=4,'core'=2,'zl'=4,'x'=4] {'zl','x'}, dimensions={0} | all-to-all | bytes 1048576 | tf_op jit(solution)/shard_map/all_to_all | solution.py:164
  133.8 1.8 residual.1
  135.6 17.9 %all_to_all.51 = f32[4,2,32,128]{3,2,1,0:T(8,128)S(1)} all-to-all(f32[4,2,32,128]{3,2,1,0:T(8,128)} %get-tuple-element.15), channel_id=1, replica_groups=mesh['y'=4,'zh'=4,'core'=2,'zl'=4,'x'=4] {'zh'}, dimensions={0} | all-to-all | bytes 262144 | tf_op jit(solution)/shard_map/all_to_all | solution.py:153
  153.6 11.3 %all_to_all.52 = f32[4,4,2,32,128]{4,3,2,1,0:T(8,128)S(1)} all-to-all(f32[4,4,2,32,128]{4,3,2,1,0:T(8,128)S(1)} %broadcast_in_dim.18), channel_id=1, replica_groups=mesh['y'=4,'zh'=4,'core'=2,'zl'=4,'x'=4] {'y'}, dimensions={0} | all-to-all | bytes 1048576 | tf_op jit(solution)/shard_map/all_to_all | solution.py:157
  164.9 0.0 copy-start.1
  164.9 1.9 collective-permute-start.2
  167.5 1.2 collective-permute-done.2.other
  168.7 0.0 copy-start.4
  168.7 0.0 copy-done.1
  168.7 0.8 copy-done.4
  169.5 2.4 %restrict.1 = f32[2,32,128]{2,1,0:T(8,128)} custom-call(s32[1]{0:T(128)} %bitcast.2.core, s32[1]{0:T(128)} %bitcast.23.count, s32[16]{0:T(128)} %bitcast.47, s32[16]{0:T(128)} %bitcast.48, f32[32,32,128]{2,1,0:T(8,128)} %bitcast.29, f32[32,32,128]{2,1,0:T(8,128)} %copy-done.4, f32[16,128,128]{2,1,0:T(8,128)} %bitcast.34, f32[2,32,128]{2,1,0:T(8,128)} %get-tuple-element.16.rest_0_), custom_call_target="tpu_custom_call" | custom-call | tf_op jit(solution)/shard_map/restrict/pallas_call | solution.py:141
  171.9 0.8 broadcast_in_dim.38
  172.7 20.1 %all_to_all.53.parts = f32[16,2,32,128]{3,2,1,0:T(8,128)} all-to-all(f32[16,2,32,128]{3,2,1,0:T(8,128)S(1)} %broadcast_in_dim.38), channel_id=1, replica_groups=mesh['y'=4,'zh'=4,'core'=2,'zl'=4,'x'=4] {'zl','x'}, dimensions={0} | all-to-all | bytes 1048576 | tf_op jit(solution)/shard_map/all_to_all | solution.py:227
  192.8 1.7 coarse.1
  (3 shorter events, 0.1 us)
Async XLA Ops:
  42.5 3.8 %copy-start = (f32[4,4,2,32,128]{4,3,2,1,0:T(8,128)}, f32[4,4,2,32,128]{4,3,2,1,0:T(8,128)S(1)}, u32[]{:S(2)}) copy-start(f32[4,4,2,32,128]{4,3,2,1,0:T(8,128)S(1)} %all_to_all.46) | copy-start | bytes 1572868
  42.5 3.8 %collective-permute-start = (f32[32,32,128]{2,1,0:T(8,128)S(1)}, f32[32,32,128]{2,1,0:T(8,128)S(1)}, u32[]{:S(2)}, u32[]{:S(2)}) collective-permute-start(f32[32,32,128]{2,1,0:T(8,128)S(1)} %bitcast.26), channel_id=1, source_target_pairs={{0,16},{16,0},{1,17},{17,1},{2,18},{18,2},{3,19},{19,3},{4,20},{20... | collective-permute-start | bytes 1572872 | tf_op jit(solution)/shard_map/ppermute | solution.py:158
  46.3 0.8 copy-start.3
  104.4 3.8 %copy-start.2 = (f32[4,4,2,32,128]{4,3,2,1,0:T(8,128)}, f32[4,4,2,32,128]{4,3,2,1,0:T(8,128)S(1)}, u32[]{:S(2)}) copy-start(f32[4,4,2,32,128]{4,3,2,1,0:T(8,128)S(1)} %all_to_all.49) | copy-start | bytes 1572868
  104.4 3.8 %collective-permute-start.1 = (f32[32,32,128]{2,1,0:T(8,128)S(1)}, f32[32,32,128]{2,1,0:T(8,128)S(1)}, u32[]{:S(2)}, u32[]{:S(2)}) collective-permute-start(f32[32,32,128]{2,1,0:T(8,128)S(1)} %bitcast.30), channel_id=1, source_target_pairs={{0,16},{16,0},{1,17},{17,1},{2,18},{18,2},{3,19},{19,3},{4,20},{20... | collective-permute-start | bytes 1572872 | tf_op jit(solution)/shard_map/ppermute | solution.py:158
  108.2 0.8 copy-start.5
  164.9 3.8 %copy-start.1 = (f32[4,4,2,32,128]{4,3,2,1,0:T(8,128)}, f32[4,4,2,32,128]{4,3,2,1,0:T(8,128)S(1)}, u32[]{:S(2)}) copy-start(f32[4,4,2,32,128]{4,3,2,1,0:T(8,128)S(1)} %all_to_all.52) | copy-start | bytes 1572868
  164.9 3.8 %collective-permute-start.2 = (f32[32,32,128]{2,1,0:T(8,128)S(1)}, f32[32,32,128]{2,1,0:T(8,128)S(1)}, u32[]{:S(2)}, u32[]{:S(2)}) collective-permute-start(f32[32,32,128]{2,1,0:T(8,128)S(1)} %bitcast.28), channel_id=1, source_target_pairs={{0,16},{16,0},{1,17},{17,1},{2,18},{18,2},{3,19},{19,3},{4,20},{20... | collective-permute-start | bytes 1572872 | tf_op jit(solution)/shard_map/ppermute | solution.py:158
  168.7 0.8 copy-start.4
